TPU v7x, 32 devices: a whole 2x2x4 slice. The times are simulated.
32 devices in a mesh: groups: 2 (over y), row: 2 (over x), col: 4 (over z), dp: 2 (over core).
Axes of the slice: x: 2, y: 2, z: 4, core: 2. Of those that a mesh axis runs over, the one named last changes fastest.
Arguments:
- features: bfloat16 [4, 512, 6144], P(('groups', 'dp'), 'row', 'col'), parts along dimension 0, may hold values from -6 to 6
- output_gradient: bfloat16 [4, 512, 6144], P(('groups', 'dp'), 'row', 'col'), parts along dimension 0, may hold values from -6 to 6
- value_weight: bfloat16 [6144, 6144], P('row', 'col'), may hold values from -0.109375 to 0.109375
- gate_weight: bfloat16 [6144, 6144], P('row', 'col'), may hold values from -1 to 1
- mixer_weight: bfloat16 [6144, 6144], P('row', 'col'), may hold values from -0.109375 to 0.109375
- conv_kernel: float32 [31, 6144], P(None, 'col'), may hold values from -1 to 1
- layer_norm_gain: float32 [6144], replicated, may hold values from 0.3 to 4.2
Outputs:
- module_out: bfloat16 [4, 512, 6144], P(('groups', 'dp'), 'row', 'col'), parts along dimension 0
- input_gradient: bfloat16 [4, 512, 6144], P(('groups', 'dp'), 'row', 'col'), parts along dimension 0
- value_weight_grad: float32 [12288, 6144], P(('groups', 'row', 'dp'), 'col'), parts along dimension 0
- gate_weight_grad: float32 [12288, 6144], P(('groups', 'row', 'dp'), 'col'), parts along dimension 0
- mixer_weight_grad: float32 [12288, 6144], P(('groups', 'row', 'dp'), 'col'), parts along dimension 0
- kernel_grad: float32 [62, 6144], P('groups', 'col'), parts along dimension 0
- norm_gain_gradient: float32 [12288], P(('groups', 'col')), parts along dimension 0
There are 2 independent parts, one for each index of `groups`. A program takes and returns all parts, laid end to end along the dimension named above; an argument that names none is the same for every part. Nothing has to cross between parts.
All inputs are finite; a program needn't handle non-finite values.
Results may differ from a plain program's by a relative error of at most 0.02.
Values may be sent and summed in bfloat16 or wider, within the bound.
A program may use at most 320 MiB of HBM per device.

v0:
```python
import jax
import jax.numpy as jnp
from jax import lax
from jax.sharding import PartitionSpec as P

MODEL_WIDTH = 6144
KERNEL = 31


EPS = 1e-05
CONTRACT_LAST = (((1,), (1,)), ((), ()))
CONTRACT_FIRST = (((0,), (0,)), ((), ()))


def with_halo(cells, sides, width):
    for axis, dim in sides:
        count = lax.axis_size(axis)
        ends = count - 1
        head = lax.slice_in_dim(cells, 0, width, axis=dim)
        tail = lax.slice_in_dim(cells, cells.shape[dim] - width, cells.shape[dim], axis=dim)
        cells = jnp.concatenate(
            [
                lax.ppermute(tail, axis, [(i, (i + 1) % count) for i in range(ends)]),
                cells,
                lax.ppermute(head, axis, [((i + 1) % count, i) for i in range(ends)]),
            ],
            axis=dim,
        )
    return cells


def shards(
    features, output_gradient, value_weight, gate_weight, mixer_weight, conv_kernel, layer_norm_gain
):
    utts, frames, column_span = features.shape
    row_span = utts * frames
    half = KERNEL // 2
    column_offset = lax.axis_index("col") * column_span
    full_input = lax.all_gather(features, "col", axis=2, tiled=True)
    feat_float = full_input.astype(jnp.float32)
    row_average = jnp.mean(feat_float, -1, keepdims=True)
    centered_input = feat_float - row_average
    variance = jnp.mean(centered_input * centered_input, -1, keepdims=True)
    inverse_deviation = lax.rsqrt(variance + EPS)
    standardized_input = centered_input * inverse_deviation
    normalized_rows = (
        (standardized_input * layer_norm_gain).astype(jnp.bfloat16).reshape(row_span, MODEL_WIDTH)
    )
    standardized_local = lax.dynamic_slice_in_dim(standardized_input, column_offset, column_span, 2)
    gain_own = lax.dynamic_slice_in_dim(layer_norm_gain, column_offset, column_span, 0)
    value_full, gate_full = (
        lax.all_gather(value_weight, "row", axis=0, tiled=True),
        lax.all_gather(gate_weight, "row", axis=0, tiled=True),
    )
    value = jnp.dot(normalized_rows, value_full, preferred_element_type=jnp.float32)
    gate = jnp.dot(normalized_rows, gate_full, preferred_element_type=jnp.float32)
    sig_gate = jax.nn.sigmoid(gate)
    glu = (value * sig_gate).astype(jnp.bfloat16).reshape(utts, frames, column_span)
    glu_pad = with_halo(glu, (("row", 1),), half)
    conv = jnp.zeros((utts, frames, column_span), jnp.float32)
    for kernel_tap in range(KERNEL):
        conv = conv + conv_kernel[kernel_tap] * glu_pad[:, kernel_tap : kernel_tap + frames].astype(
            jnp.float32
        )
    sig_conv = jax.nn.sigmoid(conv)
    mixed = (conv * sig_conv).astype(jnp.bfloat16)
    mixed_full = lax.all_gather(mixed, "col", axis=2, tiled=True).reshape(row_span, MODEL_WIDTH)
    mixer_full = lax.all_gather(mixer_weight, "row", axis=0, tiled=True)
    projected = jnp.dot(mixed_full, mixer_full, preferred_element_type=jnp.float32)
    own_input = features.astype(jnp.float32)
    module_out = (own_input + projected.reshape(utts, frames, column_span)).astype(jnp.bfloat16)
    grad_rows = output_gradient.reshape(row_span, column_span)
    mixed_grad = (
        lax.psum_scatter(
            lax.dot_general(
                mixer_full, grad_rows, CONTRACT_LAST, preferred_element_type=jnp.float32
            ).astype(jnp.bfloat16),
            "col",
            scatter_dimension=0,
            tiled=True,
        )
        .astype(jnp.float32)
        .T.reshape(utts, frames, column_span)
    )
    swish_slope = sig_conv * (1.0 + conv * (1.0 - sig_conv))
    conv_grad = (mixed_grad * swish_slope).astype(jnp.bfloat16)
    grad_pad = with_halo(conv_grad, (("row", 1),), half)
    glu_grad = jnp.zeros((utts, frames, column_span), jnp.float32)
    conv_grad_float = conv_grad.astype(jnp.float32)
    kernel_rows = []
    for kernel_tap in range(KERNEL):
        back = 2 * half - kernel_tap
        glu_grad = glu_grad + conv_kernel[kernel_tap] * grad_pad[:, back : back + frames].astype(
            jnp.float32
        )
        kernel_rows.append(
            jnp.sum(
                glu_pad[:, kernel_tap : kernel_tap + frames].astype(jnp.float32) * conv_grad_float,
                axis=(0, 1),
            )
        )
    kernel_part = jnp.stack(kernel_rows)
    glu_grad = glu_grad.reshape(row_span, column_span)
    value_grad = (glu_grad * sig_gate).astype(jnp.bfloat16)
    gate_grad = (glu_grad * value * sig_gate * (1.0 - sig_gate)).astype(jnp.bfloat16)
    grad_pair = jnp.concatenate([value_grad, gate_grad], axis=1)
    first = lax.dot_general(
        value_full, value_grad, CONTRACT_LAST, preferred_element_type=jnp.float32
    )
    second = lax.dot_general(
        gate_full, gate_grad, CONTRACT_LAST, preferred_element_type=jnp.float32
    )
    normalized_gradient_local = (
        lax.psum_scatter(
            (first + second).astype(jnp.bfloat16), "col", scatter_dimension=0, tiled=True
        )
        .astype(jnp.float32)
        .T.reshape(utts, frames, column_span)
    )
    scaled_rows = normalized_gradient_local * gain_own
    gradient_sum_local, projected_sum_local = lax.psum(
        (jnp.sum(scaled_rows, -1), jnp.sum(scaled_rows * standardized_local, -1)), "col"
    )
    back_own = (
        scaled_rows
        - gradient_sum_local[..., None] / MODEL_WIDTH
        - standardized_local * (projected_sum_local[..., None] / MODEL_WIDTH)
    ) * inverse_deviation
    pair_grad = lax.psum_scatter(
        lax.dot_general(
            normalized_rows, grad_pair, CONTRACT_FIRST, preferred_element_type=jnp.float32
        ).astype(jnp.bfloat16),
        ("row", "dp"),
        scatter_dimension=0,
        tiled=True,
    ).astype(jnp.float32)
    input_gradient = (output_gradient.astype(jnp.float32) + back_own).astype(jnp.bfloat16)
    gain_gradient_piece = jnp.sum(normalized_gradient_local * standardized_local, axis=(0, 1))
    mixer_weight_grad = lax.psum_scatter(
        lax.dot_general(
            mixed_full, grad_rows, CONTRACT_FIRST, preferred_element_type=jnp.float32
        ).astype(jnp.bfloat16),
        ("row", "dp"),
        scatter_dimension=0,
        tiled=True,
    ).astype(jnp.float32)
    kernel_grad, norm_gain_gradient = (
        lax.psum(kernel_part.astype(jnp.bfloat16), ("row", "dp")).astype(jnp.float32),
        lax.psum(gain_gradient_piece.astype(jnp.bfloat16), ("row", "dp")).astype(jnp.float32),
    )
    value_weight_grad = pair_grad[:, :column_span]
    gate_weight_grad = pair_grad[:, column_span:]
    return (
        module_out,
        input_gradient,
        value_weight_grad,
        gate_weight_grad,
        mixer_weight_grad,
        kernel_grad,
        norm_gain_gradient,
    )


def solution(mesh):
    placed = (
        P(("groups", "dp"), "row", "col"),
        P(("groups", "dp"), "row", "col"),
        P("row", "col"),
        P("row", "col"),
        P("row", "col"),
        P(None, "col"),
        P(),
    )
    return jax.shard_map(
        shards,
        mesh=mesh,
        in_specs=placed,
        out_specs=(
            P(("groups", "dp"), "row", "col"),
            P(("groups", "dp"), "row", "col"),
            P(("groups", "row", "dp"), "col"),
            P(("groups", "row", "dp"), "col"),
            P(("groups", "row", "dp"), "col"),
            P("groups", "col"),
            P(("groups", "col")),
        ),
        check_vma=False,
    )
```

profile of v0, /device:TPU:0, one launch (start us, length us, event | category | flops | bytes accessed | tf_op | source)
XLA Modules:
  0.0 1439.2 jit_solution(1543698312051208225)
XLA Ops:
  10.0 226.6 %all-gather.14.cloned.1.call-done = bf16[6144,1536]{1,0:T(8,128)(2,1)} async-done(((bf16[3072,1536]{1,0:T(8,128)(2,1)}), bf16[6144,1536]{1,0:T(8,128)(2,1)}) %all-gather.14.cloned.1.call-update) | async-done | bytes 18874384 | tf_op jit(solution)/shard_map/all_gather | solution.py:68
  236.6 19.9 %convolution_convert_fusion.2 = bf16[6144,256]{0,1:T(8,128)(2,1)} fusion(bf16[6144,1536]{1,0:T(8,128)(2,1)} %all-gather.14.cloned.1.call-done, bf16[1,256,1536]{2,1,0:T(8,128)(2,1)S(1)} %copy-done.6), kind=kOutput, calls=%fused_computation.38 | convolution fusion | flops 4833411072 | bytes 22806528 | tf_op jit(solution)/shard_map/dot_general | solution.py:75
  258.3 43.3 %all-gather.6.cloned.1.call-done = bf16[1,256,6144]{2,1,0:T(8,128)(2,1)} async-done(((bf16[1,256,1536]{2,1,0:T(8,128)(2,1)}), bf16[1,256,6144]{2,1,0:T(8,128)(2,1)}) %all-gather.6.cloned.1.call-update) | async-done | bytes 3145744 | tf_op jit(solution)/shard_map/all_gather | solution.py:39
  301.7 2.5 convert_reduce_fusion
  305.5 220.8 %all-gather.10.cloned.1.call-done = bf16[6144,1536]{1,0:T(8,128)(2,1)} async-done(((bf16[3072,1536]{1,0:T(8,128)(2,1)}), bf16[6144,1536]{1,0:T(8,128)(2,1)}) %all-gather.10.cloned.1.call-update) | async-done | bytes 18874384 | tf_op jit(solution)/shard_map/all_gather | solution.py:53
  526.3 10.6 fusion.17
  536.9 215.1 %all-gather.8.cloned.1.call-done = bf16[6144,1536]{1,0:T(8,128)(2,1)} async-done(((bf16[3072,1536]{1,0:T(8,128)(2,1)}), bf16[6144,1536]{1,0:T(8,128)(2,1)}) %all-gather.8.cloned.1.call-update) | async-done | bytes 18874384 | tf_op jit(solution)/shard_map/all_gather | solution.py:52
  752.0 10.8 multiply_convert_fusion.2
  765.0 4.7 collective-permute-start
  771.3 43.9 %reduce-scatter.5.cloned.1.call-done = bf16[1536,256]{0,1:T(8,128)(2,1)} async-done(((bf16[6144,256]{0,1:T(8,128)(2,1)}), bf16[1536,256]{0,1:T(8,128)(2,1)}) %reduce-scatter.5.cloned.1.call-update) | async-done | bytes 786448 | tf_op jit(solution)/shard_map/reduce_scatter | solution.py:74
  815.2 41.6 %fusion.111 = (bf16[1536]{0:T(1024)(128)(2,1)}, bf16[1536]{0:T(1024)(128)(2,1)}, bf16[1536]{0:T(1024)(128)(2,1)}, bf16[1536]{0:T(1024)(128)(2,1)}, bf16[1536]{0:...) fusion(bf16[1,15,1536]{2,1,0:T(8,128)(2,1)S(1)} %collective-per, ...), kind=kLoop, calls=%fused_computation.235 | loop fusion | flops 95537664 | bytes 5028864 | tf_op jit(solution)/shard_map/reduce_sum | solution.py:97
  859.8 3.4 collective-permute-start.3
  864.4 4.8 fusion.110
  869.3 2.1 fusion.95
  885.9 5.1 stack.159
  891.5 23.0 %fusion.119 = (bf16[256,1536]{1,0:T(8,128)(2,1)S(1)}, f32[1,256,1536]{2,1,0:T(8,128)S(1)}) fusion(f32[256,1536]{1,0:T(8,128)} %fusion.17, f32[256,1536]{1,0:T(8,128)} %get-tuple-element.84, bf16[1,256,1536]{2,1,0:T(8,128)(2,1)} %get-tuple-element.73, bf16[1,15,1536]{2,1,0:T(8,128)(2,1)S(1)} %collective-permute-done.3, f32[1536]{0:T(1024)S(1)} %copy-done.30, ...), kind=kLoop, calls=%fused_computation.246 | loop fusion | flops 73531392 | bytes 6574080 | tf_op jit(solution)/shard_map/convert_element_type | solution.py:105
  914.8 12.0 fusion.189
  926.8 12.1 fusion.3
  939.0 10.6 convolution_convert_fusion.1
  950.3 17.9 %convolution_convert_fusion = bf16[6144,3072]{1,0:T(8,128)(2,1)} fusion(bf16[256,1536]{1,0:T(8,128)(2,1)} %copy-done.8, bf16[256,1536]{1,0:T(8,128)(2,1)} %copy-done.9, f32[6144]{0:T(1024)S(1)} %copy-done.10, f32[256]{0:T(256)S(1)} %copy-done.33, f32[256]{0:T(256)S(1)} %copy-done.35, bf16[1,256,6144]{2,1,0:T(8,128)(2,1)S(1)} %copy-done), kind=kOutput, calls=%fused_computation | convolution fusion | flops 9693560832 | bytes 42493952 | tf_op jit(solution)/shard_map/dot_general | solution.py:130
  968.3 3.8 fusion.1
  972.2 1.6 convert_element_type.368
  973.8 10.9 fusion.18
  984.6 33.6 %reduce-scatter.7.cloned.1.call-done = bf16[1536,256]{0,1:T(8,128)(2,1)} async-done(((bf16[6144,256]{0,1:T(8,128)(2,1)}), bf16[1536,256]{0,1:T(8,128)(2,1)}) %reduce-scatter.7.cloned.1.call-update) | async-done | bytes 786448 | tf_op jit(solution)/shard_map/reduce_scatter | solution.py:114
  1018.2 2.2 fusion.64
  1020.3 6.2 psum.31
  1027.4 11.2 all-reduce
  1038.6 3.2 fusion.60
  1041.8 116.7 %reduce-scatter.11.cloned.1.call-done = bf16[1536,1536]{1,0:T(8,128)(2,1)} async-done(((bf16[6144,1536]{1,0:T(8,128)(2,1)}), bf16[1536,1536]{1,0:T(8,128)(2,1)}) %reduce-scatter.11.cloned.1.call-update) | async-done | bytes 4718608 | tf_op jit(solution)/shard_map/reduce_scatter | solution.py:139
  1158.5 7.4 convert_element_type.366
  1165.9 252.7 %reduce-scatter.9.cloned.1.call-done = bf16[1536,3072]{1,0:T(8,128)(2,1)} async-done(((bf16[6144,3072]{1,0:T(8,128)(2,1)}), bf16[1536,3072]{1,0:T(8,128)(2,1)}) %reduce-scatter.9.cloned.1.call-update) | async-done | bytes 9437200 | tf_op jit(solution)/shard_map/reduce_scatter | solution.py:129
  1418.6 13.3 fusion.186
  (163 shorter events, 30.4 us)
Async XLA Ops:
  7.2 229.5 %all-gather.14.cloned.1.call-start = ((), (), s32[]{:S(2)}) async-start(), calls=%async_computation.8 | async-start | bytes 28311552 | tf_op jit(solution)/shard_map/all_gather | solution.py:68
  7.9 293.8 %all-gather.6.cloned.1.call-start = ((), (), s32[]{:S(2)}) async-start(), calls=%async_computation.4 | async-start | bytes 3932160 | tf_op jit(solution)/shard_map/all_gather | solution.py:39
  8.6 517.6 %all-gather.10.cloned.1.call-start = ((), (), s32[]{:S(2)}) async-start(), calls=%async_computation.6 | async-start | bytes 28311552 | tf_op jit(solution)/shard_map/all_gather | solution.py:53
  9.4 227.2 %copy-start.6 = (bf16[1,256,1536]{2,1,0:T(8,128)(2,1)S(1)}, bf16[1,256,1536]{2,1,0:T(8,128)(2,1)}, u32[]{:S(2)}) copy-start(bf16[1,256,1536]{2,1,0:T(8,128)(2,1)} %param.8) | copy-start | bytes 2359300
  9.4 742.6 %all-gather.8.cloned.1.call-start = ((), (), s32[]{:S(2)}) async-start(), calls=%async_computation.5 | async-start | bytes 28311552 | tf_op jit(solution)/shard_map/all_gather | solution.py:52
  10.0 805.2 %reduce-scatter.5.cloned.1.call-start = ((), (), s32[]{:S(2)}) async-start(), calls=%async_computation.9 | async-start | bytes 3932160 | tf_op jit(solution)/shard_map/reduce_scatter | solution.py:74
  256.5 682.5 %all-gather.12.cloned.1.call-start = ((), (), s32[]{:S(2)}) async-start(), calls=%async_computation.7 | async-start | bytes 3932160 | tf_op jit(solution)/shard_map/all_gather | solution.py:67
  304.5 447.5 %copy-start.34 = (f32[256]{0:T(256)}, f32[256]{0:T(256)S(1)}, u32[]{:S(2)}) copy-start(f32[256]{0:T(256)S(1)} %broadcast_multiply_fusion.2) | copy-start | bytes 3076
  304.5 221.7 %copy-start.10 = (f32[6144]{0:T(1024)S(1)}, f32[6144]{0:T(1024)}, u32[]{:S(2)}) copy-start(f32[6144]{0:T(1024)} %param.13) | copy-start | bytes 73732
  305.5 446.5 %copy-start.32 = (f32[256]{0:T(256)}, f32[256]{0:T(256)S(1)}, u32[]{:S(2)}) copy-start(f32[256]{0:T(256)S(1)} %add_rsqrt_fusion) | copy-start | bytes 3076
  763.7 6.8 collective-permute-start.1
  765.0 6.3 collective-permute-start
  858.1 114.0 %all-reduce.3.cloned.1.call-start = ((), (), s32[]{:S(2)}) async-start(), calls=%async_computation.13 | async-start | bytes 196608 | tf_op jit(solution)/shard_map/psum | solution.py:148
  859.8 31.5 %collective-permute-start.3 = (bf16[1,15,1536]{2,1,0:T(8,128)(2,1)}, bf16[1,15,1536]{2,1,0:T(8,128)(2,1)S(1)}, u32[]{:S(2)}, u32[]{:S(2)}) collective-permute-start(bf16[1,15,1536]{2,1,0:T(8,128)(2,1)} %get-tuple-element.80), channel_id=1, source_target_pairs={{0,8},{1,9},{2,10},{3,11},{4,12},{5,13},{6,14},{7,15},{16,24},{17,... | collective-permute-start | bytes 138248 | tf_op jit(solution)/shard_map/ppermute | solution.py:23
  863.1 28.2 %collective-permute-start.2 = (bf16[1,15,1536]{2,1,0:T(8,128)(2,1)}, bf16[1,15,1536]{2,1,0:T(8,128)(2,1)}, u32[]{:S(2)}, u32[]{:S(2)}) collective-permute-start(bf16[1,15,1536]{2,1,0:T(8,128)(2,1)} %get-tuple-element.79), channel_id=1, source_target_pairs={{8,0},{9,1},{10,2},{11,3},{12,4},{13,5},{14,6},{15,7},{24,16},{25,... | collective-permute-start | bytes 138248 | tf_op jit(solution)/shard_map/ppermute | solution.py:25
  871.5 19.9 %copy-start.12 = (f32[1536]{0:T(1024)S(1)}, f32[1536]{0:T(1024)}, u32[]{:S(2)}) copy-start(f32[1536]{0:T(1024)} %get-tuple-element.51) | copy-start | bytes 18436
  871.5 19.9 %copy-start.13 = (f32[1536]{0:T(1024)S(1)}, f32[1536]{0:T(1024)}, u32[]{:S(2)}) copy-start(f32[1536]{0:T(1024)} %get-tuple-element.52) | copy-start | bytes 18436
  871.5 19.9 %copy-start.14 = (f32[1536]{0:T(1024)S(1)}, f32[1536]{0:T(1024)}, u32[]{:S(2)}) copy-start(f32[1536]{0:T(1024)} %get-tuple-element.53) | copy-start | bytes 18436
  871.5 19.9 %copy-start.15 = (f32[1536]{0:T(1024)S(1)}, f32[1536]{0:T(1024)}, u32[]{:S(2)}) copy-start(f32[1536]{0:T(1024)} %get-tuple-element.54) | copy-start | bytes 18436
  871.5 19.9 %copy-start.16 = (f32[1536]{0:T(1024)S(1)}, f32[1536]{0:T(1024)}, u32[]{:S(2)}) copy-start(f32[1536]{0:T(1024)} %get-tuple-element.55) | copy-start | bytes 18436
  871.5 19.9 %copy-start.17 = (f32[1536]{0:T(1024)S(1)}, f32[1536]{0:T(1024)}, u32[]{:S(2)}) copy-start(f32[1536]{0:T(1024)} %get-tuple-element.56) | copy-start | bytes 18436
  871.5 19.9 %copy-start.18 = (f32[1536]{0:T(1024)S(1)}, f32[1536]{0:T(1024)}, u32[]{:S(2)}) copy-start(f32[1536]{0:T(1024)} %get-tuple-element.57) | copy-start | bytes 18436
  871.5 19.9 %copy-start.19 = (f32[1536]{0:T(1024)S(1)}, f32[1536]{0:T(1024)}, u32[]{:S(2)}) copy-start(f32[1536]{0:T(1024)} %get-tuple-element.58) | copy-start | bytes 18436
  871.5 19.9 %copy-start.20 = (f32[1536]{0:T(1024)S(1)}, f32[1536]{0:T(1024)}, u32[]{:S(2)}) copy-start(f32[1536]{0:T(1024)} %get-tuple-element.59) | copy-start | bytes 18436
  871.5 19.9 %copy-start.21 = (f32[1536]{0:T(1024)S(1)}, f32[1536]{0:T(1024)}, u32[]{:S(2)}) copy-start(f32[1536]{0:T(1024)} %get-tuple-element.60) | copy-start | bytes 18436
  871.6 19.9 %copy-start.22 = (f32[1536]{0:T(1024)S(1)}, f32[1536]{0:T(1024)}, u32[]{:S(2)}) copy-start(f32[1536]{0:T(1024)} %get-tuple-element.61) | copy-start | bytes 18436
  871.6 19.9 %copy-start.23 = (f32[1536]{0:T(1024)S(1)}, f32[1536]{0:T(1024)}, u32[]{:S(2)}) copy-start(f32[1536]{0:T(1024)} %get-tuple-element.62) | copy-start | bytes 18436
  891.0 127.1 %reduce-scatter.7.cloned.1.call-start = ((), (), s32[]{:S(2)}) async-start(), calls=%async_computation.10 | async-start | bytes 3932160 | tf_op jit(solution)/shard_map/reduce_scatter | solution.py:114
  891.5 23.0 %copy-start.5 = (f32[256,1536]{1,0:T(8,128)S(1)}, f32[256,1536]{1,0:T(8,128)}, u32[]{:S(2)}) copy-start(f32[256,1536]{1,0:T(8,128)} %fusion.17) | copy-start | bytes 4718596
  939.0 219.6 %reduce-scatter.11.cloned.1.call-start = ((), (), s32[]{:S(2)}) async-start(), calls=%async_computation.12 | async-start | bytes 23592960 | tf_op jit(solution)/shard_map/reduce_scatter | solution.py:139
  949.7 469.0 %reduce-scatter.9.cloned.1.call-start = ((), (), s32[]{:S(2)}) async-start(), calls=%async_computation.11 | async-start | bytes 47185920 | tf_op jit(solution)/shard_map/reduce_scatter | solution.py:129
  984.6 54.0 %copy-start.7 = (bf16[1,256,1536]{2,1,0:T(8,128)(2,1)S(1)}, bf16[1,256,1536]{2,1,0:T(8,128)(2,1)}, u32[]{:S(2)}) copy-start(bf16[1,256,1536]{2,1,0:T(8,128)(2,1)} %param.8) | copy-start | bytes 2359300
  (27 other events, 314.4 us)
Sparse Core Ops, SparseCore 0:
  9.5 227.0 all-gather.13
  238.2 63.4 all-gather.5
  303.2 222.9 all-gather.9
  527.7 224.3 all-gather.7
  754.8 60.3 reduce-scatter.4
  858.2 63.3 all-gather.11
  924.5 30.2 all-reduce.2
  957.7 60.3 reduce-scatter.6
  1020.8 137.6 reduce-scatter.10
  1161.0 257.6 reduce-scatter.8
where the time goes:
time: 1450 us; the launch traced here: 1440 us
  waiting for transfers between devices  1160 us (80%)
  matrix products  105 us (7%)
  other arithmetic  97.1 us (7%)
  local copies, waits for them, and re-layouts  36.9 us (3%)
  blocking collectives  17.4 us (1%)
  between operations  15.3 us (1%)
    reduce_scatter x1, waiting for transfers between devices, shards(): lax.psum_scatter(lax.dot_general(normalized_rows, grad_pair, CONTRACT_FIR...  253 us
    all_gather x1, waiting for transfers between devices, shards(): mixer_full = lax.all_gather(mixer_weight, 'row', axis=0, tiled=True)  227 us
    all_gather x1, waiting for transfers between devices, shards(): lax.all_gather(gate_weight, 'row', axis=0, tiled=True)  221 us
    all_gather x1, waiting for transfers between devices, shards(): lax.all_gather(value_weight, 'row', axis=0, tiled=True)  215 us
    reduce_scatter x1, waiting for transfers between devices, shards(): lax.psum_scatter(lax.dot_general(mixed_full, grad_rows, CONTRACT_FIRST, p...  117 us
    reduce_sum x4, other arithmetic, shards(): jnp.sum(glu_pad[:, kernel_tap:kernel_tap + frames].astype(jnp.float32) *...  50 us
    reduce_scatter x1, waiting for transfers between devices, shards(): lax.psum_scatter(lax.dot_general(mixer_full, grad_rows, CONTRACT_LAST, pr...  43.9 us
    all_gather x1, waiting for transfers between devices, shards(): full_input = lax.all_gather(features, 'col', axis=2, tiled=True)  43.3 us
  transfers between devices with their start and end apart: 14, of which 9 were waited for; matrix products, arithmetic and copies ran while one was open for 13% of the time, Pallas kernels for 0%

commit v1 on v0

v1 whole, which is shorter than its diff:
```python
import jax
import jax.numpy as jnp
from jax import lax
from jax.sharding import PartitionSpec as P

EPS = 1e-05
CONTRACT_LAST = (((1,), (1,)), ((), ()))
CONTRACT_FIRST = (((0,), (0,)), ((), ()))
BF16 = jnp.bfloat16
F32 = jnp.float32


def ring(count, shift):
    return [(i, (i + shift) % count) for i in range(count)]


def gather_over(x, axis):
    count, me = lax.axis_size(axis), lax.axis_index(axis)
    pieces = [x] + [lax.ppermute(x, axis, ring(count, s)) for s in range(1, count)]
    ordered = []
    for j in range(count):
        back = (me - j) % count
        block = pieces[0]
        for s in range(1, count):
            block = jnp.where(back == s, pieces[s], block)
        ordered.append(block)
    return ordered


def scatter_over(part, axis, dim, dtype):
    count, me = lax.axis_size(axis), lax.axis_index(axis)
    width = part.shape[dim] // count
    total = lax.dynamic_slice_in_dim(part, me * width, width, dim)
    for s in range(1, count):
        sent = lax.dynamic_slice_in_dim(part, ((me + s) % count) * width, width, dim)
        total = total + lax.ppermute(sent.astype(dtype), axis, ring(count, s)).astype(F32)
    return total


def spread_over(x, axis, dim):
    count, me = lax.axis_size(axis), lax.axis_index(axis)
    width = x.shape[dim] // count
    blocks = [lax.dynamic_slice_in_dim(x, me * width, width, dim)]
    for s in range(1, count):
        sent = lax.dynamic_slice_in_dim(x, ((me + s) % count) * width, width, dim)
        blocks.append(lax.ppermute(sent, axis, ring(count, s)))
    return jnp.concatenate(blocks, axis=0)


def collect_over(x, axis):
    count = lax.axis_size(axis)
    return jnp.concatenate(
        [x] + [lax.ppermute(x, axis, ring(count, s)) for s in range(1, count)], axis=0
    )


def shards(
    features, output_gradient, value_weight, gate_weight, mixer_weight, conv_kernel, layer_norm_gain
):
    utts, frames, width = features.shape
    taps = conv_kernel.shape[0]
    half = taps // 2
    model = layer_norm_gain.shape[0]
    n_row, n_col = lax.axis_size("row"), lax.axis_size("col")
    row, col = lax.axis_index("row"), lax.axis_index("col")
    per_row = n_col // n_row
    depth = per_row * width
    narrow = width // n_row
    span = n_row * frames
    cells = utts * span
    turned = [
        (r * n_col + h * per_row + i, h * n_col + r * per_row + i)
        for r in range(n_row)
        for h in range(n_row)
        for i in range(per_row)
    ]

    def turn(x):
        return lax.ppermute(x, ("row", "col"), turned)

    own = features.astype(F32)
    block_mean = jnp.mean(own, -1)
    block_square = jnp.sum((own - block_mean[..., None]) ** 2, -1)
    stats = lax.all_gather(jnp.stack([block_mean, block_square]), ("row", "col"), axis=0)
    stats = stats.reshape(n_row, n_col, 2, utts, frames)
    mean = jnp.mean(stats[:, :, 0], 1)
    square = jnp.sum(stats[:, :, 1] + width * (stats[:, :, 0] - mean[:, None]) ** 2, 1)
    inverse = lax.rsqrt(square / model + EPS)
    mean_own = lax.dynamic_index_in_dim(mean, row, 0, keepdims=False)[..., None]
    inverse_own = lax.dynamic_index_in_dim(inverse, row, 0, keepdims=False)[..., None]
    mean_all, inverse_all = (
        jnp.swapaxes(s, 0, 1)[:, :, :, None, None] for s in (mean, inverse)
    )

    inputs = lax.all_gather(turn(features), "col", axis=0)
    inputs = inputs.reshape(n_row, per_row, utts, frames, width).transpose(2, 0, 3, 1, 4)
    gain_rows = lax.dynamic_slice_in_dim(layer_norm_gain, row * depth, depth, 0)
    normed = (
        ((inputs.astype(F32) - mean_all) * inverse_all * gain_rows.reshape(per_row, width))
        .astype(BF16)
        .reshape(cells, depth)
    )
    gate_part = jnp.dot(normed, gate_weight, preferred_element_type=F32)
    gate = scatter_over(gate_part, "row", 1, GATE_DTYPE)
    value_part = jnp.dot(normed, value_weight, preferred_element_type=F32)
    value = scatter_over(value_part, "row", 1, BF16)

    grad_rows = jnp.stack(gather_over(output_gradient, "row"), axis=1).reshape(cells, width)
    mixed_part = lax.dot_general(
        grad_rows, mixer_weight, CONTRACT_LAST, preferred_element_type=F32
    ).astype(BF16)
    mixed_part = mixed_part.reshape(cells, per_row, n_row, narrow).transpose(2, 1, 0, 3)
    mixed_grad = turn(
        lax.psum_scatter(
            mixed_part.reshape(n_col * cells, narrow), "col", scatter_dimension=0, tiled=True
        )
    )
    mixed_grad = mixed_grad.astype(F32).reshape(utts, span, narrow)

    kernel_own = lax.dynamic_slice_in_dim(conv_kernel, row * narrow, narrow, 1)
    sig_gate = jax.nn.sigmoid(gate)
    glu = (value * sig_gate).astype(BF16).reshape(utts, span, narrow)
    glu_pad = jnp.pad(glu, ((0, 0), (half, half), (0, 0)))
    conv = jnp.zeros((utts, span, narrow), F32)
    for tap in range(taps):
        conv = conv + kernel_own[tap] * glu_pad[:, tap : tap + span].astype(F32)
    sig_conv = jax.nn.sigmoid(conv)
    mixed = (conv * sig_conv).astype(BF16)
    conv_grad = (mixed_grad * (sig_conv * (1.0 + conv * (1.0 - sig_conv)))).astype(BF16)

    grad_pad = jnp.pad(conv_grad, ((0, 0), (half, half), (0, 0)))
    conv_grad_float = conv_grad.astype(F32)
    glu_grad = jnp.zeros((utts, span, narrow), F32)
    kernel_rows = []
    for tap in range(taps):
        back = 2 * half - tap
        glu_grad = glu_grad + kernel_own[tap] * grad_pad[:, back : back + span].astype(F32)
        kernel_rows.append(
            jnp.sum(glu_pad[:, tap : tap + span].astype(F32) * conv_grad_float, axis=(0, 1))
        )
    glu_grad = glu_grad.reshape(cells, narrow)
    value_grad = (glu_grad * sig_gate).astype(BF16)
    gate_grad = (glu_grad * value * sig_gate * (1.0 - sig_gate)).astype(BF16)
    value_grad, gate_grad = (
        jnp.concatenate(gather_over(g, "row"), axis=1) for g in (value_grad, gate_grad)
    )

    normed_part = (
        lax.dot_general(value_grad, value_weight, CONTRACT_LAST, preferred_element_type=F32)
        + lax.dot_general(gate_grad, gate_weight, CONTRACT_LAST, preferred_element_type=F32)
    ).astype(BF16)
    normed_part = normed_part.reshape(utts, n_row, frames, per_row, width).transpose(1, 3, 0, 2, 4)
    normed_grad = turn(
        lax.psum_scatter(
            normed_part.reshape(n_col * utts * frames, width),
            "col",
            scatter_dimension=0,
            tiled=True,
        )
    )
    normed_grad = normed_grad.astype(F32).reshape(utts, frames, width)

    mixed_rows = lax.all_gather(turn(mixed), "col", axis=0)
    mixed_rows = (
        mixed_rows.reshape(n_row, per_row, utts, span, narrow)
        .transpose(2, 3, 1, 0, 4)
        .reshape(cells, depth)
    )
    projected = jnp.dot(mixed_rows, mixer_weight, preferred_element_type=F32)
    projected = scatter_over(projected.reshape(utts, span, width), "row", 1, BF16)
    module_out = (own + projected).astype(BF16)

    normed_cells = spread_over(normed, "dp", 1)
    value_weight_grad, gate_weight_grad = (
        lax.dot_general(
            normed_cells, collect_over(g, "dp"), CONTRACT_FIRST, preferred_element_type=F32
        )
        for g in (value_grad, gate_grad)
    )
    mixer_weight_grad = lax.dot_general(
        spread_over(mixed_rows, "dp", 1),
        collect_over(grad_rows, "dp"),
        CONTRACT_FIRST,
        preferred_element_type=F32,
    )
    kernel_parts = lax.all_gather(jnp.stack(kernel_rows), ("row", "dp"), axis=0)
    kernel_parts = kernel_parts.reshape(n_row, -1, taps, narrow)
    kernel_grad = jnp.sum(kernel_parts, 1).transpose(1, 0, 2).reshape(taps, width)

    standardized = (own - mean_own) * inverse_own
    gain_own = lax.dynamic_slice_in_dim(layer_norm_gain, col * width, width, 0)
    scaled = normed_grad * gain_own
    sums = lax.psum(jnp.stack([jnp.sum(scaled, -1), jnp.sum(scaled * standardized, -1)]), "col")
    input_gradient = (
        output_gradient.astype(F32)
        + (scaled - sums[0][..., None] / model - standardized * (sums[1][..., None] / model))
        * inverse_own
    ).astype(BF16)
    norm_gain_gradient = lax.psum(jnp.sum(normed_grad * standardized, axis=(0, 1)), ("row", "dp"))
    return (
        module_out,
        input_gradient,
        value_weight_grad,
        gate_weight_grad,
        mixer_weight_grad,
        kernel_grad,
        norm_gain_gradient,
    )


GATE_DTYPE = F32


def solution(mesh):
    placed = (
        P(("groups", "dp"), "row", "col"),
        P(("groups", "dp"), "row", "col"),
        P("row", "col"),
        P("row", "col"),
        P("row", "col"),
        P(None, "col"),
        P(),
    )
    return jax.shard_map(
        shards,
        mesh=mesh,
        in_specs=placed,
        out_specs=(
            P(("groups", "dp"), "row", "col"),
            P(("groups", "dp"), "row", "col"),
            P(("groups", "row", "dp"), "col"),
            P(("groups", "row", "dp"), "col"),
            P(("groups", "row", "dp"), "col"),
            P("groups", "col"),
            P(("groups", "col")),
        ),
        check_vma=False,
    )
```

time: 1450 us -> 476 us (0.33)
  waiting for transfers between devices: 1160 us -> 79.3 us
  starting transfers between devices: 11.5 us -> 124 us
  blocking collectives: 17.4 us -> 78.1 us
  other arithmetic: 97.1 us -> 51.1 us
  matrix products: 105 us -> 78.1 us
    all_gather x5 -> x2, waiting for transfers between devices: 706 us -> 0.02 us  [the longest x1 0.02 us: shards(): inputs = lax.all_gather(turn(features), 'col', axis=0)]
    reduce_scatter x4 -> x2, waiting for transfers between devices: 447 us -> 29 us  [the longest x1 29 us: shards(): lax.psum_scatter(mixed_part.reshape(n_col * cells, narrow), 'col', scatte...]
    ppermute x4 -> x15, starting transfers between devices: 10.7 us -> 123 us  [the longest x3 106 us: gather_over(): lax.ppermute(x, axis, ring(count, s))]
    ppermute x4 -> x15, waiting for transfers between devices: 0.77 us -> 50.2 us  [the longest x3 50.2 us: gather_over(): lax.ppermute(x, axis, ring(count, s))]
    reduce_sum x8 -> x11, other arithmetic: 55.9 us -> 16.5 us  [the longest x4 15 us: shards(): jnp.sum(glu_pad[:, tap:tap + span].astype(F32) * conv_grad_float, axis=(0...]
    all_gather x0 -> x2, blocking collectives: none -> 34.7 us  [the longest x1 28 us: shards(): lax.all_gather(jnp.stack([block_mean, block_square]), ('row', 'col'), axi...]
    dot_general x8 -> x9, matrix products: 105 us -> 78.1 us  [the longest x2 25.4 us: shards(): lax.dot_general(normed_cells, collect_over(g, 'dp'), CONTRACT_FIRST, pref...]
    psum x2, blocking collectives: 17.4 us -> 43.4 us  [the longest x1 37 us: shards(): lax.psum(jnp.stack([jnp.sum(scaled, -1), jnp.sum(scaled * standardized, -...]
  transfers between devices with their start and end apart: 14 -> 19, of which waited for: 9 -> 4; matrix products, arithmetic and copies ran while one was open for 13% -> 33% of each run, Pallas kernels for 0% -> 0%
where the time goes in v1:
time: 476 us; the launch traced here: 470 us
  starting transfers between devices  124 us (26%)
  waiting for transfers between devices  79.3 us (17%)
  matrix products  78.1 us (16%)
  blocking collectives  78.1 us (16%)
  other arithmetic  51.1 us (11%)
  local copies, waits for them, and re-layouts  45.2 us (9%)
  between operations  14.8 us (3%)
    ppermute x3, starting transfers between devices, gather_over(): lax.ppermute(x, axis, ring(count, s))  106 us
    ppermute x3, waiting for transfers between devices, gather_over(): lax.ppermute(x, axis, ring(count, s))  50.2 us
    psum x1, blocking collectives, shards(): lax.psum(jnp.stack([jnp.sum(scaled, -1), jnp.sum(scaled * standardized, -...  37 us
    reduce_scatter x1, waiting for transfers between devices, shards(): lax.psum_scatter(mixed_part.reshape(n_col * cells, narrow), 'col', scatte...  29 us
    all_gather x1, blocking collectives, shards(): lax.all_gather(jnp.stack([block_mean, block_square]), ('row', 'col'), axi...  28 us
    dot_general x2, matrix products, shards(): lax.dot_general(normed_cells, collect_over(g, 'dp'), CONTRACT_FIRST, pref...  25.4 us
    reduce_sum x4, other arithmetic, shards(): jnp.sum(glu_pad[:, tap:tap + span].astype(F32) * conv_grad_float, axis=(0...  15 us
    ppermute x4, starting transfers between devices, turn(): return lax.ppermute(x, ('row', 'col'), turned)  12.5 us
  transfers between devices with their start and end apart: 19, of which 4 were waited for; matrix products, arithmetic and copies ran while one was open for 33% of the time, Pallas kernels for 0%

profile of v1, /device:TPU:0, one launch (start us, length us, event | category | flops | bytes accessed | tf_op | source)
XLA Modules:
  0.0 470.5 jit_solution(16571329316580543862)
XLA Ops:
  10.0 41.3 %collective-permute-start.5 = (bf16[1,256,1536]{2,1,0:T(8,128)(2,1)}, bf16[1,256,1536]{2,1,0:T(8,128)(2,1)S(1)}, u32[]{:S(2)}, u32[]{:S(2)}) collective-permute-start(bf16[1,256,1536]{2,1,0:T(8,128)(2,1)} %param.8), channel_id=1, source_target_pairs={{0,8},{8,0},{1,9},{9,1},{2,10},{10,2},{3,11},{11,3},{4,12},{12,4},... | collective-permute-start | bytes 2359304 | tf_op jit(solution)/shard_map/ppermute | solution.py:19
  51.2 16.9 %collective-permute-done.5 = bf16[1,256,1536]{2,1,0:T(8,128)(2,1)S(1)} collective-permute-done((bf16[1,256,1536]{2,1,0:T(8,128)(2,1)}, bf16[1,256,1536]{2,1,0:T(8,128)(2,1)S(1)}, u32[]{:S(2)}, u32[]{:S(2)}) %collective-permute-start.5) | collective-permute-done | bytes 786464 | tf_op jit(solution)/shard_map/ppermute | solution.py:19
  70.7 10.3 %convolution_convert_fusion = bf16[512,3072]{1,0:T(8,128)(2,1)} fusion(bf16[512,1536]{1,0:T(8,128)(2,1)S(1)} %bitcast.137, bf16[3072,1536]{1,0:T(8,128)(2,1)} %param.11), kind=kOutput, calls=%fused_computation.37 | convolution fusion | flops 4833411072 | bytes 14155776 | tf_op jit(solution)/shard_map/dot_general | solution.py:109
  81.0 7.1 %reshape.322 = bf16[512,2,2,768]{3,2,1,0:T(2,128)(2,1)S(1)} reshape(bf16[512,3072]{1,0:T(8,128)(2,1)} %convolution_convert_fusion) | data formatting | bytes 6291456 | tf_op jit(solution)/shard_map/reshape | solution.py:112
  91.9 28.0 %all-gather.1 = f32[16,1,256]{2,1,0:T(1,128)S(1)} all-gather(f32[2,1,256]{2,1,0:T(1,128)S(1)} %pad_maximum_fusion.6), channel_id=3, replica_groups=mesh['groups'=2,'row'=2,'col'=4,'dp'=2] {'row','col'}, dimensions={0}, use_global_device_ids=true | all-gather | bytes 18432 | tf_op jit(solution)/shard_map/all_gather | solution.py:84
  120.0 3.5 convert.6
  123.5 6.1 %fusion.2 = bf16[2,2,1,256,1536]{4,1,3,0,2:T(2,128)(2,1)S(1)} fusion(f32[2,2,1,256,1536]{4,3,1,0,2:T(8,128)S(1)} %convert.6, f32[2,1536]{1,0:T(2,128)S(1)} %mul.735, f32[2,256]{1,0:T(2,128)S(1)} %add_rsqrt_fusion, f32[2,256]{1,0:T(2,128)S(1)} %broadcast_multiply_fusion), kind=kLoop, calls=%fused_computation.36 | loop fusion | flops 6291456 | bytes 9453568 | tf_op jit(solution)/shard_map/convert.2
  130.4 5.0 %fusion.136 = f32[512,1536]{1,0:T(8,128)S(1)} fusion(bf16[512,3072]{1,0:T(8,128)(2,1)S(1)} %bitcast.129, bf16[3072,1536]{1,0:T(8,128)(2,1)S(1)} %bitcast.157), kind=kOutput, calls=%fused_computation.281 | convolution fusion | flops 4831838208 | bytes 15728640 | tf_op jit(solution)/shard_map/dot_general | solution.py:103
  139.4 5.0 %fusion.135 = f32[512,1536]{1,0:T(8,128)S(1)} fusion(bf16[512,3072]{1,0:T(8,128)(2,1)S(1)} %bitcast.130, bf16[3072,1536]{1,0:T(8,128)(2,1)S(1)} %bitcast.159), kind=kOutput, calls=%fused_computation.280 | convolution fusion | flops 4831838208 | bytes 15728640 | tf_op jit(solution)/shard_map/dot_general | solution.py:105
  146.5 29.0 %reduce-scatter.3.cloned.1.call-done = bf16[512,768]{1,0:T(8,128)(2,1)} async-done(((bf16[2048,768]{1,0:T(8,128)(2,1)}), bf16[512,768]{1,0:T(8,128)(2,1)}) %reduce-scatter.3.cloned.1.call-update) | async-done | bytes 786448 | tf_op jit(solution)/shard_map/reduce_scatter | solution.py:114
  175.5 7.4 %collective-permute-start.6 = (bf16[512,768]{1,0:T(8,128)(2,1)}, bf16[512,768]{1,0:T(8,128)(2,1)}, u32[]{:S(2)}, u32[]{:S(2)}) collective-permute-start(bf16[512,768]{1,0:T(8,128)(2,1)} %reduce-scatter.3.cloned.1.call-done), channel_id=1, source_target_pairs={{0,0},{2,2},{4,8},{6,10},{8,4},{10,6},{12,12},{14,14},{1,1},{3,3},... | collective-permute-start | bytes 2359304 | tf_op jit(solution)/shard_map/ppermute | solution.py:79
  186.0 2.6 multiply_convert_fusion.1
  188.6 10.0 %fusion.114 = (f32[768]{0:T(1024)S(1)}, f32[768]{0:T(1024)S(1)}, f32[768]{0:T(1024)S(1)}, f32[768]{0:T(1024)S(1)}, f32[768]{0:T(1024)S(1)}, /*index=5*/f32[768]{...) fusion(bf16[1,512,768]{2,1,0:T(8,128)(2,1)S(1)} %bitcast.123, ...), kind=kLoop, calls=%fused_computation.188 | loop fusion | flops 51111168 | bytes 4841472 | tf_op jit(solution)/shard_map/reduce_sum | solution.py:139
  201.1 8.5 %fusion.118 = (bf16[512,768]{1,0:T(8,128)(2,1)}, f32[1,512,768]{2,1,0:T(8,128)S(1)}) fusion(f32[512,768]{1,0:T(8,128)S(1)} %collective-permute-done.2, f32[512,1536]{1,0:T(8,128)} %copy-done.3, s32[]{:T(128)S(6)} %select_n.103, f32[768]{0:T(1024)S(1)} %get-tuple-element.70, f32[768]{0:T(1024)S(1)} %get-tuple-element.41, f32[768]{0:T(1024)S(1)} %get-tuple-element.42, ...), kind=kLoop, calls=%fused_computation.198 | loop fusion | flops 38535168 | bytes 6386692 | tf_op jit(solution)/shard_map/convert_element_type | solution.py:142
  209.7 2.7 fusion.121
  212.4 64.8 %collective-permute-start.8 = (bf16[512,768]{1,0:T(8,128)(2,1)}, bf16[512,768]{1,0:T(8,128)(2,1)}, u32[]{:S(2)}, u32[]{:S(2)}) collective-permute-start(bf16[512,768]{1,0:T(8,128)(2,1)} %fusion.121), channel_id=1, source_target_pairs={{0,8},{8,0},{1,9},{9,1},{2,10},{10,2},{3,11},{11,3},{4,12},{12,4},... | collective-permute-start | bytes 2359304 | tf_op jit(solution)/shard_map/ppermute | solution.py:19
  277.3 18.5 %collective-permute-done.8 = bf16[512,768]{1,0:T(8,128)(2,1)} collective-permute-done((bf16[512,768]{1,0:T(8,128)(2,1)}, bf16[512,768]{1,0:T(8,128)(2,1)}, u32[]{:S(2)}, u32[]{:S(2)}) %collective-permute-start.8) | collective-permute-done | bytes 786464 | tf_op jit(solution)/shard_map/ppermute | solution.py:19
  297.3 14.7 %collective-permute-done.7 = bf16[512,768]{1,0:T(8,128)(2,1)} collective-permute-done((bf16[512,768]{1,0:T(8,128)(2,1)}, bf16[512,768]{1,0:T(8,128)(2,1)}, u32[]{:S(2)}, u32[]{:S(2)}) %collective-permute-start.7) | collective-permute-done | bytes 786464 | tf_op jit(solution)/shard_map/ppermute | solution.py:19
  313.8 8.3 %fusion.131 = f32[512,3072]{1,0:T(8,128)S(1)} fusion(bf16[3072,1536]{1,0:T(8,128)(2,1)} %param.10, bf16[512,768]{1,0:T(8,128)(2,1)S(1)} %get-tuple-element.82, bf16[512,768]{1,0:T(8,128)(2,1)S(1)} %get-tuple-element.81), kind=kOutput, calls=%fused_computation.279 | convolution fusion | flops 4834983936 | bytes 17301504 | tf_op jit(solution)/shard_map/dot_general | solution.py:150
  322.1 6.4 %add_convert_fusion = bf16[512,3072]{1,0:T(8,128)(2,1)} fusion(f32[512,3072]{1,0:T(8,128)S(1)} %fusion.131, bf16[3072,1536]{1,0:T(8,128)(2,1)S(1)} %bitcast.161, bf16[512,768]{1,0:T(8,128)(2,1)S(1)} %get-tuple-element.80, bf16[512,768]{1,0:T(8,128)(2,1)S(1)} %get-tuple-element.79), kind=kOutput, calls=%fused_computation.35 | convolution fusion | flops 4838129664 | bytes 20447232 | tf_op jit(solution)/shard_map/dot_general | solution.py:149
  328.6 8.3 %reshape.327 = bf16[1,2,256,2,1536]{4,3,2,1,0:T(2,128)(2,1)} reshape(bf16[512,3072]{1,0:T(8,128)(2,1)} %add_convert_fusion) | data formatting | bytes 6291456 | tf_op jit(solution)/shard_map/reshape | solution.py:152
  336.8 4.1 copy.40
  340.9 3.9 constant_dynamic-slice_fusion.4
  353.5 6.7 %all-gather.4 = f32[4,31,768]{2,1,0:T(8,128)S(1)} all-gather(f32[1,31,768]{2,1,0:T(8,128)S(1)} %bitcast.142), channel_id=5, replica_groups=mesh['groups'=2,'row'=2,'col'=4,'dp'=2] {'row','dp'}, dimensions={0}, use_global_device_ids=true | all-gather | bytes 476160 | tf_op jit(solution)/shard_map/all_gather | solution.py:186
  361.2 13.1 %fusion.3 = f32[1536,1536]{1,0:T(8,128)} fusion(bf16[512,1536]{1,0:T(8,128)(2,1)} %collective-permute-done.11, bf16[512,768]{1,0:T(8,128)(2,1)S(1)} %copy-done.12, bf16[512,768]{1,0:T(8,128)(2,1)S(1)} %copy-done.9, bf16[512,1536]{1,0:T(8,128)(2,1)} %collective-permute-done.10, bf16[512,1536]{1,0:T(8,128)(2,1)} %get-tuple-element.77), kind=kOutput, calls=%fused_computation.39 | convolution fusion | flops 4847566848 | bytes 15728640 | tf_op jit(solution)/shard_map/dot_general | solution.py:175
  374.3 12.3 %fusion.9 = f32[1536,1536]{1,0:T(8,128)} fusion(bf16[512,1536]{1,0:T(8,128)(2,1)} %collective-permute-done.12, bf16[512,768]{1,0:T(8,128)(2,1)S(1)} %get-tuple-element.82, bf16[512,768]{1,0:T(8,128)(2,1)S(1)} %get-tuple-element.81, bf16[512,1536]{1,0:T(8,128)(2,1)} %collective-permute-done.10, bf16[512,1536]{1,0:T(8,128)(2,1)S(1)} %copy-done.18), kind=kOutput, calls=%fused_computation.45 | convolution fusion | flops 4847566848 | bytes 15728640 | tf_op jit(solution)/shard_map/dot_general | solution.py:175
  386.7 3.2 copy.38
  392.1 7.7 %fusion.137 = f32[512,1536]{1,0:T(8,128)S(1)} fusion(bf16[512,3072]{0,1:T(8,128)(2,1)S(1)} %bitcast.133, bf16[3072,1536]{1,0:T(8,128)(2,1)} %param.11), kind=kOutput, calls=%fused_computation.282 | convolution fusion | flops 4831838208 | bytes 15728640 | tf_op jit(solution)/shard_map/dot_general | solution.py:169
  405.9 9.8 %fusion.15 = f32[1536,1536]{1,0:T(8,128)} fusion(bf16[512,1536]{0,1:T(8,128)(2,1)} %collective-permute-done.13, bf16[512,1536]{0,1:T(8,128)(2,1)} %get-tuple-element.75, bf16[512,1536]{1,0:T(8,128)(2,1)} %collective-permute-done.14, bf16[512,1536]{1,0:T(8,128)(2,1)S(1)} %bitcast.139), kind=kOutput, calls=%fused_computation.51 | convolution fusion | flops 4844421120 | bytes 15728640 | tf_op jit(solution)/shard_map/dot_general | solution.py:180
  416.7 37.0 %psum.14 = f32[2,1,256]{2,1,0:T(1,128)S(1)} all-reduce(f32[2,1,256]{2,1,0:T(1,128)S(1)} %pad_maximum_fusion.7), channel_id=1, replica_groups=mesh['groups'=2,'row'=2,'col'=4,'dp'=2] {'col'}, use_global_device_ids=true, to_apply=%region_8.9 | all-reduce | flops 512 | bytes 4096 | tf_op jit(solution)/shard_map/psum | solution.py:193
  453.6 6.4 %psum.15 = f32[1536]{0:T(1024)} all-reduce(f32[1536]{0:T(1024)S(1)} %get-tuple-element.7), channel_id=1, replica_groups=mesh['groups'=2,'row'=2,'col'=4,'dp'=2] {'row','dp'}, use_global_device_ids=true, to_apply=%region_42.43 | all-reduce | flops 1536 | bytes 12288 | tf_op jit(solution)/shard_map/psum | solution.py:199
  460.1 3.7 fusion.62
  (168 shorter events, 43.3 us)
Async XLA Ops:
  7.2 112.8 %all-gather.8.cloned.1.call-start = ((), (), s32[]{:S(2)}) async-start(), calls=%async_computation.4 | async-start | bytes 3932160 | tf_op jit(solution)/shard_map/all_gather | solution.py:95
  7.2 1.8 collective-permute-start
  9.9 165.6 %reduce-scatter.3.cloned.1.call-start = ((), (), s32[]{:S(2)}) async-start(), calls=%async_computation.2 | async-start | bytes 3932160 | tf_op jit(solution)/shard_map/reduce_scatter | solution.py:114
  10.0 58.2 %collective-permute-start.5 = (bf16[1,256,1536]{2,1,0:T(8,128)(2,1)}, bf16[1,256,1536]{2,1,0:T(8,128)(2,1)S(1)}, u32[]{:S(2)}, u32[]{:S(2)}) collective-permute-start(bf16[1,256,1536]{2,1,0:T(8,128)(2,1)} %param.8), channel_id=1, source_target_pairs={{0,8},{8,0},{1,9},{9,1},{2,10},{10,2},{3,11},{11,3},{4,12},{12,4},... | collective-permute-start | bytes 2359304 | tf_op jit(solution)/shard_map/ppermute | solution.py:19
  90.2 296.5 %all-gather.10.cloned.1.call-start = ((), (), s32[]{:S(2)}) async-start(), calls=%async_computation.5 | async-start | bytes 3932160 | tf_op jit(solution)/shard_map/all_gather | solution.py:163
  120.0 10.4 %slice-start = ((s8[9437184]{0:T(1024)(128)(4,1)}), s8[4194304]{0:T(1024)(128)(4,1)S(1)}, s32[]{:S(2)}) async-start(s8[9437184]{0:T(1024)(128)(4,1)} %bitcast.156), calls=%async_computation.6 | async-start | bytes 8388608
  120.0 10.4 %slice-start.1 = ((s8[9437184]{0:T(1024)(128)(4,1)}), s8[4194304]{0:T(1024)(128)(4,1)S(1)}, s32[]{:S(2)}) async-start(s8[9437184]{0:T(1024)(128)(4,1)} %bitcast.156), calls=%async_computation.7 | async-start | bytes 8388608
  129.6 9.8 %slice-start.3 = ((s8[9437184]{0:T(1024)(128)(4,1)}), s8[4194304]{0:T(1024)(128)(4,1)S(1)}, s32[]{:S(2)}) async-start(s8[9437184]{0:T(1024)(128)(4,1)} %bitcast.158), calls=%async_computation.9 | async-start | bytes 8388608
  130.3 9.1 %copy-start = (bf16[64,8,2,1536]{3,1,2,0:T(8,128)(2,1)}, bf16[64,8,2,1536]{3,1,2,0:T(8,128)(2,1)S(1)}, u32[]{:S(2)}) copy-start(bf16[64,8,2,1536]{3,1,2,0:T(8,128)(2,1)S(1)} %copy.43) | copy-start | bytes 9437188
  130.4 9.0 %slice-start.4 = ((s8[9437184]{0:T(1024)(128)(4,1)}), s8[4194304]{0:T(1024)(128)(4,1)S(1)}, s32[]{:S(2)}) async-start(s8[9437184]{0:T(1024)(128)(4,1)} %bitcast.158), calls=%async_computation.10 | async-start | bytes 8388608
  130.4 9.0 %slice-start.5 = ((s8[9437184]{0:T(1024)(128)(4,1)}), s8[1048576]{0:T(1024)(128)(4,1)S(1)}, s32[]{:S(2)}) async-start(s8[9437184]{0:T(1024)(128)(4,1)} %bitcast.158), calls=%async_computation.11 | async-start | bytes 2097152
  137.6 48.4 %collective-permute-start.2 = (f32[512,768]{1,0:T(8,128)}, f32[512,768]{1,0:T(8,128)S(1)}, u32[]{:S(2)}, u32[]{:S(2)}) collective-permute-start(f32[512,768]{1,0:T(8,128)} %constant_dynamic-slice_fusion.7), channel_id=1, source_target_pairs={{0,8},{8,0},{1,9},{9,1},{2,10},{10,2},{3,11},{11,3},{4,12},{12,4},... | collective-permute-start | bytes 4718600 | tf_op jit(solution)/shard_map/ppermute | solution.py:36
  146.2 39.7 %collective-permute-start.1 = (bf16[512,768]{1,0:T(8,128)(2,1)S(1)}, bf16[512,768]{1,0:T(8,128)(2,1)S(1)}, u32[]{:S(2)}, u32[]{:S(2)}) collective-permute-start(bf16[512,768]{1,0:T(8,128)(2,1)S(1)} %dynamic-slice_convert_fusion.1), channel_id=1, source_target_pairs={{0,8},{8,0},{1,9},{9,1},{2,10},{10,2},{3,11},{11,3},{4,12},{12,4},... | collective-permute-start | bytes 2359304 | tf_op jit(solution)/shard_map/ppermute | solution.py:36
  175.5 13.1 %collective-permute-start.6 = (bf16[512,768]{1,0:T(8,128)(2,1)}, bf16[512,768]{1,0:T(8,128)(2,1)}, u32[]{:S(2)}, u32[]{:S(2)}) collective-permute-start(bf16[512,768]{1,0:T(8,128)(2,1)} %reduce-scatter.3.cloned.1.call-done), channel_id=1, source_target_pairs={{0,0},{2,2},{4,8},{6,10},{8,4},{10,6},{12,12},{14,14},{1,1},{3,3},... | collective-permute-start | bytes 2359304 | tf_op jit(solution)/shard_map/ppermute | solution.py:79
  199.1 1.6 collective-permute-start.3
  200.7 203.5 %reduce-scatter.5.cloned.1.call-start = ((), (), s32[]{:S(2)}) async-start(), calls=%async_computation.3 | async-start | bytes 3932160 | tf_op jit(solution)/shard_map/reduce_scatter | solution.py:154
  201.1 8.6 %copy-start.4 = (f32[512,1536]{1,0:T(8,128)S(1)}, f32[512,1536]{1,0:T(8,128)}, u32[]{:S(2)}) copy-start(f32[512,1536]{1,0:T(8,128)} %copy-done.3) | copy-start | bytes 9437188
  201.1 8.6 %copy-start.6 = (f32[512,1536]{1,0:T(8,128)S(1)}, f32[512,1536]{1,0:T(8,128)}, u32[]{:S(2)}) copy-start(f32[512,1536]{1,0:T(8,128)} %copy-done.5) | copy-start | bytes 9437188
  212.4 83.5 %collective-permute-start.8 = (bf16[512,768]{1,0:T(8,128)(2,1)}, bf16[512,768]{1,0:T(8,128)(2,1)}, u32[]{:S(2)}, u32[]{:S(2)}) collective-permute-start(bf16[512,768]{1,0:T(8,128)(2,1)} %fusion.121), channel_id=1, source_target_pairs={{0,8},{8,0},{1,9},{9,1},{2,10},{10,2},{3,11},{11,3},{4,12},{12,4},... | collective-permute-start | bytes 2359304 | tf_op jit(solution)/shard_map/ppermute | solution.py:19
  277.2 34.9 %collective-permute-start.7 = (bf16[512,768]{1,0:T(8,128)(2,1)}, bf16[512,768]{1,0:T(8,128)(2,1)}, u32[]{:S(2)}, u32[]{:S(2)}) collective-permute-start(bf16[512,768]{1,0:T(8,128)(2,1)} %get-tuple-element.73), channel_id=1, source_target_pairs={{0,8},{8,0},{1,9},{9,1},{2,10},{10,2},{3,11},{11,3},{4,12},{12,4},... | collective-permute-start | bytes 2359304 | tf_op jit(solution)/shard_map/ppermute | solution.py:19
  277.3 128.6 %collective-permute-start.14 = (bf16[512,1536]{1,0:T(8,128)(2,1)}, bf16[512,1536]{1,0:T(8,128)(2,1)}, u32[]{:S(2)}, u32[]{:S(2)}) collective-permute-start(bf16[512,1536]{1,0:T(8,128)(2,1)} %bitcast.138), channel_id=1, source_target_pairs={{0,1},{1,0},{2,3},{3,2},{4,5},{5,4},{6,7},{7,6},{8,9},{9,8},{10,11... | collective-permute-start | bytes 4718600 | tf_op jit(solution)/shard_map/ppermute | solution.py:53
  312.1 10.0 %slice-start.6 = ((s8[9437184]{0:T(1024)(128)(4,1)}), s8[4194304]{0:T(1024)(128)(4,1)S(1)}, s32[]{:S(2)}) async-start(s8[9437184]{0:T(1024)(128)(4,1)} %bitcast.160), calls=%async_computation.12 | async-start | bytes 8388608
  313.7 8.3 %slice-start.7 = ((s8[9437184]{0:T(1024)(128)(4,1)}), s8[4194304]{0:T(1024)(128)(4,1)S(1)}, s32[]{:S(2)}) async-start(s8[9437184]{0:T(1024)(128)(4,1)} %bitcast.160), calls=%async_computation.13 | async-start | bytes 8388608
  344.8 16.4 %collective-permute-start.10 = (bf16[512,1536]{1,0:T(8,128)(2,1)}, bf16[512,1536]{1,0:T(8,128)(2,1)}, u32[]{:S(2)}, u32[]{:S(2)}) collective-permute-start(bf16[512,1536]{1,0:T(8,128)(2,1)} %get-tuple-element.78), channel_id=1, source_target_pairs={{0,1},{1,0},{2,3},{3,2},{4,5},{5,4},{6,7},{7,6},{8,9},{9,8},{10,11... | collective-permute-start | bytes 4718600 | tf_op jit(solution)/shard_map/ppermute | solution.py:46
  346.1 15.1 %collective-permute-start.11 = (bf16[512,1536]{1,0:T(8,128)(2,1)}, bf16[512,1536]{1,0:T(8,128)(2,1)}, u32[]{:S(2)}, u32[]{:S(2)}) collective-permute-start(bf16[512,1536]{1,0:T(8,128)(2,1)} %pad_maximum_fusion.4), channel_id=1, source_target_pairs={{0,1},{1,0},{2,3},{3,2},{4,5},{5,4},{6,7},{7,6},{8,9},{9,8},{10,11... | collective-permute-start | bytes 4718600 | tf_op jit(solution)/shard_map/ppermute | solution.py:53
  352.1 22.2 %collective-permute-start.12 = (bf16[512,1536]{1,0:T(8,128)(2,1)}, bf16[512,1536]{1,0:T(8,128)(2,1)}, u32[]{:S(2)}, u32[]{:S(2)}) collective-permute-start(bf16[512,1536]{1,0:T(8,128)(2,1)} %pad_maximum_fusion.5), channel_id=1, source_target_pairs={{0,1},{1,0},{2,3},{3,2},{4,5},{5,4},{6,7},{7,6},{8,9},{9,8},{10,11... | collective-permute-start | bytes 4718600 | tf_op jit(solution)/shard_map/ppermute | solution.py:53
  361.2 13.1 %copy-start.18 = (bf16[512,1536]{1,0:T(8,128)(2,1)S(1)}, bf16[512,1536]{1,0:T(8,128)(2,1)}, u32[]{:S(2)}) copy-start(bf16[512,1536]{1,0:T(8,128)(2,1)} %get-tuple-element.77) | copy-start | bytes 4718596
  391.8 14.2 %collective-permute-start.13 = (bf16[512,1536]{0,1:T(8,128)(2,1)}, bf16[512,1536]{0,1:T(8,128)(2,1)}, u32[]{:S(2)}, u32[]{:S(2)}) collective-permute-start(bf16[512,1536]{0,1:T(8,128)(2,1)} %get-tuple-element.76), channel_id=1, source_target_pairs={{0,1},{1,0},{2,3},{3,2},{4,5},{5,4},{6,7},{7,6},{8,9},{9,8},{10,11... | collective-permute-start | bytes 4718600 | tf_op jit(solution)/shard_map/ppermute | solution.py:46
  402.4 57.6 %collective-permute-start.4 = (bf16[1,256,1536]{2,1,0:T(8,128)(2,1)}, bf16[1,256,1536]{2,1,0:T(8,128)(2,1)}, u32[]{:S(2)}, u32[]{:S(2)}) collective-permute-start(bf16[1,256,1536]{2,1,0:T(8,128)(2,1)} %fusion.122), channel_id=1, source_target_pairs={{0,8},{8,0},{1,9},{9,1},{2,10},{10,2},{3,11},{11,3},{4,12},{12,4},... | collective-permute-start | bytes 2359304 | tf_op jit(solution)/shard_map/ppermute | solution.py:36
  404.1 11.6 %collective-permute-start.9 = (bf16[256,1536]{1,0:T(8,128)(2,1)}, bf16[256,1536]{1,0:T(8,128)(2,1)S(1)}, u32[]{:S(2)}, u32[]{:S(2)}) collective-permute-start(bf16[256,1536]{1,0:T(8,128)(2,1)} %reduce-scatter.5.cloned.1.call-done), channel_id=1, source_target_pairs={{0,0},{2,2},{4,8},{6,10},{8,4},{10,6},{12,12},{14,14},{1,1},{3,3},... | collective-permute-start | bytes 2359304 | tf_op jit(solution)/shard_map/ppermute | solution.py:79
  405.9 10.1 %copy-start.2 = (bf16[1,256,1536]{2,1,0:T(8,128)(2,1)S(1)}, bf16[1,256,1536]{2,1,0:T(8,128)(2,1)}, u32[]{:S(2)}) copy-start(bf16[1,256,1536]{2,1,0:T(8,128)(2,1)} %param.7) | copy-start | bytes 2359300
  415.8 44.3 %copy-start.13 = (bf16[1,256,1536]{2,1,0:T(8,128)(2,1)S(1)}, bf16[1,256,1536]{2,1,0:T(8,128)(2,1)}, u32[]{:S(2)}) copy-start(bf16[1,256,1536]{2,1,0:T(8,128)(2,1)} %param.8) | copy-start | bytes 2359300
  (17 other events, 72.6 us)
Sparse Core Ops, SparseCore 0:
  10.1 103.4 all-gather.7
  116.5 58.9 reduce-scatter.2
  200.8 125.7 all-gather.9
  341.0 59.7 reduce-scatter.4
